TPU v7x, 32 devices: a whole 2x2x4 slice. The times are simulated.
32 devices in a mesh: chain: 2 (over x), slab: 16 (over z, y, core).
Axes of the slice: x: 2, y: 2, z: 4, core: 2. Of those that a mesh axis runs over, the one named last changes fastest.
Arguments:
- whitened: float32 [1024, 256, 256], P(('chain', 'slab')), parts along dimension 0, may hold values from -6 to 6
- counts: int32 [1024, 256, 256], P(('chain', 'slab')), parts along dimension 0, may hold values from 0 to 24
- exposure: int32 [1024, 256, 256], P(('chain', 'slab')), parts along dimension 0, may hold values from 1 to 12
- cholesky_east: float32 [512, 512], replicated, as said below
- cholesky_north: float32 [256, 256], replicated, as said below
- cholesky_time: float32 [256, 256], replicated, as said below
Outputs:
- gradient: float32 [1024, 256, 256], P(('chain', 'slab')), parts along dimension 0
- density: float32 [2], P('chain'), parts along dimension 0
There are 2 independent parts, one for each index of `chain`. A program takes and returns all parts, laid end to end along the dimension named above; an argument that names none is the same for every part. Nothing has to cross between parts.
Inputs may be any that keep to these rules, and one draw needn't show every extreme that they name: `cholesky_east`: lower triangular with a positive diagonal, each row of unit length. `cholesky_north`: lower triangular with a positive diagonal, each row of unit length. `cholesky_time`: lower triangular with a positive diagonal, each row of unit length.
All inputs are finite; a program needn't handle non-finite values.
Results may differ from a plain program's by a relative error of at most 0.00008.
Values sent between devices are 32-bit elements; how exact they have to be, the bound alone decides.
A program may use at most 128 MiB of HBM per device.

v0:
```python
import jax
import jax.numpy as jnp
from jax import lax
from jax.sharding import PartitionSpec as P

field_scale = 0.6


def mode_last(values, matrix):
    return jnp.einsum("abc,tc->abt", values, matrix, precision=lax.Precision.HIGHEST)


def mode_middle(values, matrix):
    return jnp.einsum("abc,yb->ayc", values, matrix, precision=lax.Precision.HIGHEST)


def mode_first(values, matrix):
    return jnp.einsum("abc,xa->xbc", values, matrix, precision=lax.Precision.HIGHEST)


def adjoint_last(values, matrix):
    return jnp.einsum("abt,tc->abc", values, matrix, precision=lax.Precision.HIGHEST)


def adjoint_middle(values, matrix):
    return jnp.einsum("ayc,yb->abc", values, matrix, precision=lax.Precision.HIGHEST)


def adjoint_first(values, matrix):
    return jnp.einsum("xbc,xa->abc", values, matrix, precision=lax.Precision.HIGHEST)


def to_lines(values):
    return lax.all_to_all(values, "slab", split_axis=1, concat_axis=0, tiled=True)


def to_planes(values):
    return lax.all_to_all(values, "slab", split_axis=0, concat_axis=1, tiled=True)


def per_device(whitened, counts, exposure, cholesky_east, cholesky_north, cholesky_time):
    cell_count = whitened.shape[0] * whitened.shape[1] * whitened.shape[2]
    prior_term = -0.5 * jnp.sum(whitened * whitened)
    partly = mode_middle(mode_last(whitened, cholesky_time), cholesky_north)
    counts_lines, exposure_lines = (
        lax.all_to_all(counts, "slab", split_axis=1, concat_axis=0, tiled=True),
        lax.all_to_all(exposure, "slab", split_axis=1, concat_axis=0, tiled=True),
    )
    log_lines = field_scale * mode_first(to_lines(partly), cholesky_east)
    observed = counts_lines.astype(jnp.float32)
    intensity = exposure_lines.astype(jnp.float32) * jnp.exp(log_lines)
    residual = observed - intensity
    partial_sum = jnp.sum(observed * log_lines - intensity) + prior_term
    adjoint_lines = adjoint_first(residual, cholesky_east)
    adjoint = to_planes(adjoint_lines)
    adjoint = adjoint_last(adjoint_middle(adjoint, cholesky_north), cholesky_time)
    gradient = field_scale * adjoint - whitened
    total_sum = lax.psum(partial_sum, "slab")
    density = total_sum / (cell_count * lax.axis_size("slab"))
    return (gradient, jnp.reshape(density, (1,)))


def solution(mesh):
    placed = (
        P(("chain", "slab"), None, None),
        P(("chain", "slab"), None, None),
        P(("chain", "slab"), None, None),
        P(),
        P(),
        P(),
    )
    return jax.shard_map(
        per_device,
        mesh=mesh,
        in_specs=placed,
        out_specs=(P(("chain", "slab"), None, None), P("chain")),
        check_vma=False,
    )
```

profile of v0, /device:TPU:16, one launch (start us, length us, event | category | flops | bytes accessed | tf_op | source)
XLA Modules:
  0.0 900.2 jit_solution(4330136956723541852)
XLA Ops:
  0.6 11.5 %copy.35 = s32[32,256,256]{2,0,1:T(8,128)} copy(s32[32,256,256]{2,1,0:T(8,128)} %param.8) | data formatting | bytes 16777216 | tf_op args[2]
  12.2 6.2 all-to-all-start.1
  18.4 11.6 %copy.32 = s32[32,256,256]{2,0,1:T(8,128)} copy(s32[32,256,256]{2,1,0:T(8,128)} %param.7) | data formatting | bytes 16777216 | tf_op args[1]
  30.0 170.9 %all-to-all-done.1 = s32[32,256,256]{2,0,1:T(8,128)} async-done(((s32[32,256,256]{2,0,1:T(8,128)}), s32[32,256,256]{2,0,1:T(8,128)}, u32[]{:S(2)}, u32[]{:S(2)}) %all-to-all-start.1) | async-done | bytes 8388640 | tf_op jit(solution)/shard_map/all_to_all | solution.py:47
  200.9 4.9 all-to-all-start
  205.9 10.7 %fusion.22 = f32[32,256,256]{1,2,0:T(8,128)S(1)} fusion(f32[32,256,256]{2,1,0:T(8,128)} %param.6, f32[256,256]{1,0:T(8,128)S(1)} %copy-done.2), kind=kOutput, calls=%fused_computation.24 | convolution fusion | flops 6442450944 | bytes 17039360 | tf_op jit(solution)/shard_map/abc,tc->abt/dot_general | solution.py:10
  216.6 8.9 convolution_bitcast_fusion
  225.5 10.3 %copy.39 = f32[32,256,256]{2,0,1:T(8,128)} copy(f32[32,256,256]{1,2,0:T(8,128)} %convolution_bitcast_fusion) | data formatting | bytes 16777216 | tf_op jit(solution)/shard_map/abc,yb->ayc/transpose | solution.py:14
  235.8 152.4 %all-to-all-done = s32[32,256,256]{2,0,1:T(8,128)} async-done(((s32[32,256,256]{2,0,1:T(8,128)}), s32[32,256,256]{2,0,1:T(8,128)}, u32[]{:S(2)}, u32[]{:S(2)}) %all-to-all-start) | async-done | bytes 8388640 | tf_op jit(solution)/shard_map/all_to_all | solution.py:46
  388.2 5.0 all-to-all-start.2
  393.2 8.2 copy_convert_fusion
  405.9 10.4 %copy.43 = f32[512,16,256]{0,2,1:T(8,128)} copy(f32[512,16,256]{2,1,0:T(8,128)} %bitcast.68) | data formatting | bytes 16777216 | tf_op jit(solution)/shard_map/convert_element_type | solution.py:51
  416.3 8.2 copy_convert_fusion.1
  428.9 10.1 %copy.44 = f32[512,16,256]{0,2,1:T(8,128)} copy(f32[512,16,256]{2,1,0:T(8,128)} %bitcast.70) | data formatting | bytes 16777216 | tf_op jit(solution)/shard_map/convert_element_type | solution.py:50
  439.0 136.6 %all-to-all-done.2 = f32[32,256,256]{2,0,1:T(8,128)} async-done(((f32[32,256,256]{2,0,1:T(8,128)}), f32[32,256,256]{2,0,1:T(8,128)}, u32[]{:S(2)}, u32[]{:S(2)}) %all-to-all-start.2) | async-done | bytes 8388640 | tf_op jit(solution)/shard_map/all_to_all | solution.py:34
  575.6 13.6 %copy.41 = f32[16,32,16,256]{3,2,1,0:T(8,128)} copy(f32[16,32,16,256]{3,1,2,0:T(8,128)} %bitcast.11) | data formatting | bytes 16777216 | tf_op jit(solution)/shard_map/all_to_all | solution.py:34
  589.2 37.1 %fusion.4 = (f32[]{:T(128)}, f32[16,256,512]{2,1,0:T(8,128)}) fusion(f32[512,16,256]{0,2,1:T(8,128)} %copy.44, f32[512,16,256]{0,2,1:T(8,128)} %copy.43, f32[512,512]{1,0:T(8,128)S(1)} %copy-done, f32[512,16,256]{2,1,0:T(8,128)} %bitcast.66), kind=kOutput, calls=%fused_computation.6 | convolution fusion | flops 12895387648 | bytes 34603012 | tf_op jit(solution)/shard_map/abc,xa->xbc/dot_general | solution.py:18
  626.3 20.3 %fusion.13 = f32[512,16,256]{0,2,1:T(8,128)} fusion(f32[512,16,256]{0,2,1:T(8,128)} %copy.44, f32[512,16,256]{0,2,1:T(8,128)S(1)} %bitcast.65, f32[16,256,512]{2,1,0:T(8,128)} %get-tuple-element.3, f32[512,512]{1,0:T(8,128)S(1)} %copy-done), kind=kOutput, calls=%fused_computation.17 | convolution fusion | flops 12891193344 | bytes 34603008 | tf_op jit(solution)/shard_map/xbc,xa->abc/dot_general | solution.py:30
  646.6 10.3 %copy.45 = f32[512,16,256]{2,1,0:T(8,128)} copy(f32[512,16,256]{0,2,1:T(8,128)} %fusion.13) | data formatting | bytes 16777216 | tf_op jit(solution)/shard_map/xbc,xa->abc/dot_general | solution.py:30
  656.8 4.6 all-to-all-start.3
  661.5 6.1 multiply_reduce_fusion
  668.9 193.6 %psum.7 = f32[]{:T(128)} all-reduce(f32[]{:T(128)S(6)} %add.5), channel_id=1, replica_groups=mesh['chain'=2,'slab'=16] {'slab'}, use_global_device_ids=true, to_apply=%region_2.0 | all-reduce | flops 1 | bytes 8 | tf_op jit(solution)/shard_map/psum | solution.py:58
  867.8 14.6 %fusion.18 = f32[32,256,256]{2,1,0:T(8,128)S(1)} fusion(f32[32,256,256]{2,1,0:T(8,128)S(1)} %bitcast.71, f32[256,256]{1,0:T(8,128)S(1)} %copy-done.1), kind=kOutput, calls=%fused_computation.20 | convolution fusion | flops 6442450944 | bytes 17039360 | tf_op jit(solution)/shard_map/ayc,yb->abc/dot_general | solution.py:26
  882.4 16.3 %multiply_subtract_fusion = f32[32,256,256]{2,1,0:T(8,128)} fusion(f32[32,256,256]{2,1,0:T(8,128)S(1)} %bitcast.63, f32[32,256,256]{2,1,0:T(8,128)S(1)} %fusion.18, f32[256,256]{1,0:T(8,128)S(1)} %copy-done.2), kind=kOutput, calls=%fused_computation.12 | convolution fusion | flops 6446645248 | bytes 25427968 | tf_op jit(solution)/shard_map/abt,tc->abc/dot_general | solution.py:22
  (20 shorter events, 13.4 us)
Async XLA Ops:
  0.6 588.6 %copy-start = (f32[512,512]{1,0:T(8,128)S(1)}, f32[512,512]{1,0:T(8,128)}, u32[]{:S(2)}) copy-start(f32[512,512]{1,0:T(8,128)} %param.9) | copy-start | bytes 3145732
  12.2 188.7 %all-to-all-start.1 = ((s32[32,256,256]{2,0,1:T(8,128)}), s32[32,256,256]{2,0,1:T(8,128)}, u32[]{:S(2)}, u32[]{:S(2)}) async-start(s32[32,256,256]{2,0,1:T(8,128)} %copy.35), calls=%async_computation.1 | async-start | bytes 16777216 | tf_op jit(solution)/shard_map/all_to_all | solution.py:47
  30.0 175.9 %copy-start.2 = (f32[256,256]{1,0:T(8,128)S(1)}, f32[256,256]{1,0:T(8,128)}, u32[]{:S(2)}) copy-start(f32[256,256]{1,0:T(8,128)} %param.11) | copy-start | bytes 786436
  200.9 187.3 %all-to-all-start = ((s32[32,256,256]{2,0,1:T(8,128)}), s32[32,256,256]{2,0,1:T(8,128)}, u32[]{:S(2)}, u32[]{:S(2)}) async-start(s32[32,256,256]{2,0,1:T(8,128)} %copy.32), calls=%async_computation | async-start | bytes 16777216 | tf_op jit(solution)/shard_map/all_to_all | solution.py:46
  205.9 10.7 %copy-start.1 = (f32[256,256]{1,0:T(8,128)S(1)}, f32[256,256]{1,0:T(8,128)}, u32[]{:S(2)}) copy-start(f32[256,256]{1,0:T(8,128)} %param.10) | copy-start | bytes 786436
  388.2 187.4 %all-to-all-start.2 = ((f32[32,256,256]{2,0,1:T(8,128)}), f32[32,256,256]{2,0,1:T(8,128)}, u32[]{:S(2)}, u32[]{:S(2)}) async-start(f32[32,256,256]{2,0,1:T(8,128)} %copy.39), calls=%async_computation.2 | async-start | bytes 16777216 | tf_op jit(solution)/shard_map/all_to_all | solution.py:34
  575.6 50.7 %slice-start.2 = ((s8[8388608]{0:T(1024)(128)(4,1)}), s8[4194304]{0:T(1024)(128)(4,1)S(1)}, s32[]{:S(2)}) async-start(s8[8388608]{0:T(1024)(128)(4,1)} %bitcast.64), calls=%async_computation.6 | async-start | bytes 8388608
  589.2 37.1 %slice-start.3 = ((s8[8388608]{0:T(1024)(128)(4,1)}), s8[4194304]{0:T(1024)(128)(4,1)S(1)}, s32[]{:S(2)}) async-start(s8[8388608]{0:T(1024)(128)(4,1)} %bitcast.64), calls=%async_computation.7 | async-start | bytes 8388608
  656.8 206.4 %all-to-all-start.3 = ((f32[512,16,256]{2,1,0:T(8,128)}), f32[512,16,256]{2,1,0:T(8,128)}, u32[]{:S(2)}, u32[]{:S(2)}) async-start(f32[512,16,256]{2,1,0:T(8,128)} %copy.45), calls=%async_computation.3 | async-start | bytes 16777216 | tf_op jit(solution)/shard_map/all_to_all | solution.py:38
  863.2 19.2 %slice-start = ((s8[8388608]{0:T(1024)(128)(4,1)}), s8[4194304]{0:T(1024)(128)(4,1)S(1)}, s32[]{:S(2)}) async-start(s8[8388608]{0:T(1024)(128)(4,1)} %bitcast.62), calls=%async_computation.4 | async-start | bytes 8388608
  867.8 14.6 %slice-start.1 = ((s8[8388608]{0:T(1024)(128)(4,1)}), s8[4194304]{0:T(1024)(128)(4,1)S(1)}, s32[]{:S(2)}) async-start(s8[8388608]{0:T(1024)(128)(4,1)} %bitcast.62), calls=%async_computation.5 | async-start | bytes 8388608
where the time goes:
time: 909 us; the launch traced here: 900 us
  waiting for transfers between devices  460 us (51%)
  blocking collectives  194 us (21%)
  matrix products  108 us (12%)
  local copies, waits for them, and re-layouts  91.2 us (10%)
  other arithmetic  22.6 us (2%)
  starting transfers between devices  20.8 us (2%)
    psum x1, blocking collectives, per_device(): total_sum = lax.psum(partial_sum, 'slab')  194 us
    all_to_all x1, waiting for transfers between devices, per_device(): lax.all_to_all(exposure, 'slab', split_axis=1, concat_axis=0, tiled=True)  171 us
    all_to_all x1, waiting for transfers between devices, per_device(): lax.all_to_all(counts, 'slab', split_axis=1, concat_axis=0, tiled=True)  152 us
    all_to_all x1, waiting for transfers between devices, to_lines(): lax.all_to_all(values, 'slab', split_axis=1, concat_axis=0, tiled=True)  137 us
    dot_general x1, matrix products, mode_first(): jnp.einsum('abc,xa->xbc', values, matrix, precision=lax.Precision.HIGHEST)  37.1 us
    unnamed x16, local copies, waits for them, and re-layouts  23.2 us
    dot_general x1, matrix products, adjoint_first(): jnp.einsum('xbc,xa->abc', values, matrix, precision=lax.Precision.HIGHEST)  20.3 us
  transfers between devices with their start and end apart: 4, of which 3 were waited for; matrix products, arithmetic and copies ran while one was open for 10% of the time, Pallas kernels for 0%

commit v1 on v0

--- a/solution.py
+++ b/solution.py
@@ -44,7 +44,12 @@
     partly = mode_middle(mode_last(whitened, cholesky_time), cholesky_north)
     counts_lines, exposure_lines = (
         lax.all_to_all(counts, "slab", split_axis=1, concat_axis=0, tiled=True),
-        lax.all_to_all(exposure, "slab", split_axis=1, concat_axis=0, tiled=True),
+        jnp.concatenate(
+            lax.all_to_all(
+                jnp.stack(jnp.split(exposure, lax.axis_size("slab"), axis=1)), "slab", 0, 0
+            ),
+            axis=0,
+        ),
     )
     log_lines = field_scale * mode_first(to_lines(partly), cholesky_east)
     observed = counts_lines.astype(jnp.float32)

time: 909 us -> 926 us (1.019)
  local copies, waits for them, and re-layouts: 91.2 us -> 105 us
    unnamed x16 -> x30, local copies, waits for them, and re-layouts: 23.2 us -> 40 us
where the time goes in v1:
time: 926 us; the launch traced here: 919 us
  waiting for transfers between devices  465 us (50%)
  blocking collectives  194 us (21%)
  matrix products  108 us (12%)
  local copies, waits for them, and re-layouts  105 us (11%)
  other arithmetic  22.3 us (2%)
  starting transfers between devices  20.9 us (2%)
    psum x1, blocking collectives, per_device(): total_sum = lax.psum(partial_sum, 'slab')  194 us
    all_to_all x1, waiting for transfers between devices, per_device(): lax.all_to_all(jnp.stack(jnp.split(exposure, lax.axis_size('slab'), axis=...  171 us
    all_to_all x1, waiting for transfers between devices, per_device(): lax.all_to_all(counts, 'slab', split_axis=1, concat_axis=0, tiled=True)  152 us
    all_to_all x1, waiting for transfers between devices, to_lines(): lax.all_to_all(values, 'slab', split_axis=1, concat_axis=0, tiled=True)  142 us
    unnamed x30, local copies, waits for them, and re-layouts  40 us
    dot_general x1, matrix products, mode_first(): jnp.einsum('abc,xa->xbc', values, matrix, precision=lax.Precision.HIGHEST)  37.1 us
    dot_general x1, matrix products, adjoint_first(): jnp.einsum('xbc,xa->abc', values, matrix, precision=lax.Precision.HIGHEST)  20.3 us
  transfers between devices with their start and end apart: 4, of which 3 were waited for; matrix products, arithmetic and copies ran while one was open for 10% of the time, Pallas kernels for 0%

profile of v1, /device:TPU:16, one launch (start us, length us, event | category | flops | bytes accessed | tf_op | source)
XLA Modules:
  0.0 918.9 jit_solution(11005668251070183937)
XLA Ops:
  30.9 6.2 all-to-all-start.1
  37.0 11.6 %copy.31 = s32[32,256,256]{2,0,1:T(8,128)} copy(s32[32,256,256]{2,1,0:T(8,128)} %param.7) | data formatting | bytes 16777216 | tf_op args[1]
  48.7 170.9 %all-to-all-done.1 = s32[16,32,16,256]{3,2,1,0:T(8,128)} async-done(((s32[16,32,16,256]{3,2,1,0:T(8,128)}), s32[16,32,16,256]{3,2,1,0:T(8,128)}, u32[]{:S(2)}, u32[]{:S(2)}) %all-to-all-start.1) | async-done | bytes 8388640 | tf_op jit(solution)/shard_map/all_to_all | solution.py:48
  219.6 5.2 all-to-all-start
  224.8 10.7 %fusion.22 = f32[32,256,256]{1,2,0:T(8,128)S(1)} fusion(f32[32,256,256]{2,1,0:T(8,128)} %param.6, f32[256,256]{1,0:T(8,128)S(1)} %copy-done.2), kind=kOutput, calls=%fused_computation.39 | convolution fusion | flops 6442450944 | bytes 17039360 | tf_op jit(solution)/shard_map/abc,tc->abt/dot_general | solution.py:10
  235.5 8.9 convolution_bitcast_fusion
  244.4 10.3 %copy.35 = f32[32,256,256]{2,0,1:T(8,128)} copy(f32[32,256,256]{1,2,0:T(8,128)} %convolution_bitcast_fusion) | data formatting | bytes 16777216 | tf_op jit(solution)/shard_map/abc,yb->ayc/transpose | solution.py:14
  254.7 152.4 %all-to-all-done = s32[32,256,256]{2,0,1:T(8,128)} async-done(((s32[32,256,256]{2,0,1:T(8,128)}), s32[32,256,256]{2,0,1:T(8,128)}, u32[]{:S(2)}, u32[]{:S(2)}) %all-to-all-start) | async-done | bytes 8388640 | tf_op jit(solution)/shard_map/all_to_all | solution.py:46
  407.2 4.9 all-to-all-start.2
  412.1 7.9 convert_element_type.22
  420.0 10.0 %copy.39 = f32[512,16,256]{0,2,1:T(8,128)} copy(f32[512,16,256]{2,1,0:T(8,128)} %bitcast.96) | data formatting | bytes 16777216 | tf_op jit(solution)/shard_map/convert_element_type | solution.py:56
  430.0 8.2 copy_convert_fusion
  442.6 10.0 %copy.40 = f32[512,16,256]{0,2,1:T(8,128)} copy(f32[512,16,256]{2,1,0:T(8,128)} %bitcast.98) | data formatting | bytes 16777216 | tf_op jit(solution)/shard_map/convert_element_type | solution.py:55
  452.6 141.9 %all-to-all-done.2 = f32[32,256,256]{2,0,1:T(8,128)} async-done(((f32[32,256,256]{2,0,1:T(8,128)}), f32[32,256,256]{2,0,1:T(8,128)}, u32[]{:S(2)}, u32[]{:S(2)}) %all-to-all-start.2) | async-done | bytes 8388640 | tf_op jit(solution)/shard_map/all_to_all | solution.py:34
  594.5 13.6 %copy.37 = f32[16,32,16,256]{3,2,1,0:T(8,128)} copy(f32[16,32,16,256]{3,1,2,0:T(8,128)} %bitcast.25) | data formatting | bytes 16777216 | tf_op jit(solution)/shard_map/all_to_all | solution.py:34
  608.1 37.1 %fusion.4 = (f32[]{:T(128)}, f32[16,256,512]{2,1,0:T(8,128)}) fusion(f32[512,16,256]{0,2,1:T(8,128)} %copy.40, f32[512,16,256]{0,2,1:T(8,128)} %copy.39, f32[512,512]{1,0:T(8,128)S(1)} %copy-done, f32[512,16,256]{2,1,0:T(8,128)} %bitcast.95), kind=kOutput, calls=%fused_computation.6 | convolution fusion | flops 12895387648 | bytes 34603012 | tf_op jit(solution)/shard_map/abc,xa->xbc/dot_general | solution.py:18
  645.2 20.3 %fusion.13 = f32[512,16,256]{0,2,1:T(8,128)} fusion(f32[512,16,256]{0,2,1:T(8,128)} %copy.40, f32[512,16,256]{0,2,1:T(8,128)S(1)} %bitcast.94, f32[16,256,512]{2,1,0:T(8,128)} %get-tuple-element.3, f32[512,512]{1,0:T(8,128)S(1)} %copy-done), kind=kOutput, calls=%fused_computation.16 | convolution fusion | flops 12891193344 | bytes 34603008 | tf_op jit(solution)/shard_map/xbc,xa->abc/dot_general | solution.py:30
  665.4 10.3 %copy.41 = f32[512,16,256]{2,1,0:T(8,128)} copy(f32[512,16,256]{0,2,1:T(8,128)} %fusion.13) | data formatting | bytes 16777216 | tf_op jit(solution)/shard_map/xbc,xa->abc/dot_general | solution.py:30
  675.7 4.6 all-to-all-start.3
  680.3 6.1 multiply_reduce_fusion
  687.8 193.6 %psum.7 = f32[]{:T(128)} all-reduce(f32[]{:T(128)S(6)} %add.5), channel_id=1, replica_groups=mesh['chain'=2,'slab'=16] {'slab'}, use_global_device_ids=true, to_apply=%region_2.0 | all-reduce | flops 1 | bytes 8 | tf_op jit(solution)/shard_map/psum | solution.py:63
  882.1 4.6 copy.42
  886.7 14.6 %fusion.18 = f32[32,256,256]{2,1,0:T(8,128)S(1)} fusion(f32[32,256,256]{2,1,0:T(8,128)S(1)} %bitcast.99, f32[256,256]{1,0:T(8,128)S(1)} %copy-done.1), kind=kOutput, calls=%fused_computation.35 | convolution fusion | flops 6442450944 | bytes 17039360 | tf_op jit(solution)/shard_map/ayc,yb->abc/dot_general | solution.py:26
  901.3 16.3 %multiply_subtract_fusion = f32[32,256,256]{2,1,0:T(8,128)} fusion(f32[32,256,256]{2,1,0:T(8,128)S(1)} %bitcast.92, f32[32,256,256]{2,1,0:T(8,128)S(1)} %fusion.18, f32[256,256]{1,0:T(8,128)S(1)} %copy-done.2), kind=kOutput, calls=%fused_computation.11 | convolution fusion | flops 6446645248 | bytes 25427968 | tf_op jit(solution)/shard_map/abt,tc->abc/dot_general | solution.py:22
  (34 shorter events, 34.6 us)
Async XLA Ops:
  0.6 607.4 %copy-start = (f32[512,512]{1,0:T(8,128)S(1)}, f32[512,512]{1,0:T(8,128)}, u32[]{:S(2)}) copy-start(f32[512,512]{1,0:T(8,128)} %param.9) | copy-start | bytes 3145732
  30.9 188.7 %all-to-all-start.1 = ((s32[16,32,16,256]{3,2,1,0:T(8,128)}), s32[16,32,16,256]{3,2,1,0:T(8,128)}, u32[]{:S(2)}, u32[]{:S(2)}) async-start(s32[16,32,16,256]{3,2,1,0:T(8,128)} %bitcast_dynamic-update-slice_fusion), calls=%async_computation.1 | async-start | bytes 16777216 | tf_op jit(solution)/shard_map/all_to_all | solution.py:48
  48.7 176.1 %copy-start.2 = (f32[256,256]{1,0:T(8,128)S(1)}, f32[256,256]{1,0:T(8,128)}, u32[]{:S(2)}) copy-start(f32[256,256]{1,0:T(8,128)} %param.11) | copy-start | bytes 786436
  219.6 187.6 %all-to-all-start = ((s32[32,256,256]{2,0,1:T(8,128)}), s32[32,256,256]{2,0,1:T(8,128)}, u32[]{:S(2)}, u32[]{:S(2)}) async-start(s32[32,256,256]{2,0,1:T(8,128)} %copy.31), calls=%async_computation | async-start | bytes 16777216 | tf_op jit(solution)/shard_map/all_to_all | solution.py:46
  224.8 10.7 %copy-start.1 = (f32[256,256]{1,0:T(8,128)S(1)}, f32[256,256]{1,0:T(8,128)}, u32[]{:S(2)}) copy-start(f32[256,256]{1,0:T(8,128)} %param.10) | copy-start | bytes 786436
  407.2 187.3 %all-to-all-start.2 = ((f32[32,256,256]{2,0,1:T(8,128)}), f32[32,256,256]{2,0,1:T(8,128)}, u32[]{:S(2)}, u32[]{:S(2)}) async-start(f32[32,256,256]{2,0,1:T(8,128)} %copy.35), calls=%async_computation.2 | async-start | bytes 16777216 | tf_op jit(solution)/shard_map/all_to_all | solution.py:34
  594.5 50.7 %slice-start.2 = ((s8[8388608]{0:T(1024)(128)(4,1)}), s8[4194304]{0:T(1024)(128)(4,1)S(1)}, s32[]{:S(2)}) async-start(s8[8388608]{0:T(1024)(128)(4,1)} %bitcast.93), calls=%async_computation.6 | async-start | bytes 8388608
  608.1 37.1 %slice-start.3 = ((s8[8388608]{0:T(1024)(128)(4,1)}), s8[4194304]{0:T(1024)(128)(4,1)S(1)}, s32[]{:S(2)}) async-start(s8[8388608]{0:T(1024)(128)(4,1)} %bitcast.93), calls=%async_computation.7 | async-start | bytes 8388608
  675.7 206.4 %all-to-all-start.3 = ((f32[512,16,256]{2,1,0:T(8,128)}), f32[512,16,256]{2,1,0:T(8,128)}, u32[]{:S(2)}, u32[]{:S(2)}) async-start(f32[512,16,256]{2,1,0:T(8,128)} %copy.41), calls=%async_computation.3 | async-start | bytes 16777216 | tf_op jit(solution)/shard_map/all_to_all | solution.py:38
  882.1 19.2 %slice-start = ((s8[8388608]{0:T(1024)(128)(4,1)}), s8[4194304]{0:T(1024)(128)(4,1)S(1)}, s32[]{:S(2)}) async-start(s8[8388608]{0:T(1024)(128)(4,1)} %bitcast.91), calls=%async_computation.4 | async-start | bytes 8388608
  886.7 14.6 %slice-start.1 = ((s8[8388608]{0:T(1024)(128)(4,1)}), s8[4194304]{0:T(1024)(128)(4,1)S(1)}, s32[]{:S(2)}) async-start(s8[8388608]{0:T(1024)(128)(4,1)} %bitcast.91), calls=%async_computation.5 | async-start | bytes 8388608
